TPU v7x, 32 devices: a whole 2x2x4 slice. The times are simulated.
32 devices in a mesh: dp: 8 (over z, y), fsdp: 4 (over x, core).
Axes of the slice: x: 2, y: 2, z: 4, core: 2. Of those that a mesh axis runs over, the one named last changes fastest.
Arguments:
- states: bfloat16 [20480, 1280], P(('dp', 'fsdp')), may hold values from -0.1796875 to 0.1796875
- teacher: float32 [20480, 1280], P(('dp', 'fsdp')), may hold values from -0.18 to 0.18
- parent_ids: int32 [160], P('dp'), may hold values from -1 to 159, as said below
- valid_mask: int32 [20480], P(('dp', 'fsdp')), may hold values from 0 to 1, as said below
- w_query: bfloat16 [1280, 1280], P(('dp', 'fsdp')), may hold values from -0.15625 to 0.15625
- w_key: bfloat16 [1280, 1280], P(('dp', 'fsdp')), may hold values from -0.15625 to 0.15625
- w_value: bfloat16 [1280, 1280], P(('dp', 'fsdp')), may hold values from -0.15625 to 0.15625
- w_out: bfloat16 [1280, 1280], P(('dp', 'fsdp')), may hold values from -0.15625 to 0.15625
- w_up: bfloat16 [1280, 5120], P(('dp', 'fsdp')), may hold values from -0.15625 to 0.15625
- w_gate: bfloat16 [1280, 5120], P(('dp', 'fsdp')), may hold values from -0.15625 to 0.15625
- w_down: bfloat16 [5120, 1280], P(('dp', 'fsdp')), may hold values from -0.078125 to 0.078125
- qk_scale: bfloat16 [1280], P(('dp', 'fsdp')), may hold values from 0.69921875 to 1.5
- attn_rate: bfloat16 [1280], P(('dp', 'fsdp')), may hold values from 0.099609375 to 0.59765625
- mlp_rate: bfloat16 [1280], P(('dp', 'fsdp')), may hold values from 0.099609375 to 0.59765625
- up_scale: bfloat16 [5120], P(('dp', 'fsdp')), may hold values from 0.5 to 2
- gate_scale: bfloat16 [5120], P(('dp', 'fsdp')), may hold values from 0.5 to 2
Outputs:
- out_states: bfloat16 [20480, 1280], P(('dp', 'fsdp'))
- loss: float32 [], replicated
- grad_states: float32 [20480, 1280], P(('dp', 'fsdp'))
- grad_query: float32 [1280, 1280], P(('dp', 'fsdp'))
- grad_key: float32 [1280, 1280], P(('dp', 'fsdp'))
- grad_value: float32 [1280, 1280], P(('dp', 'fsdp'))
- grad_out: float32 [1280, 1280], P(('dp', 'fsdp'))
- grad_up: float32 [1280, 5120], P(('dp', 'fsdp'))
- grad_gate: float32 [1280, 5120], P(('dp', 'fsdp'))
- grad_down: float32 [5120, 1280], P(('dp', 'fsdp'))
- grad_qk_scale: float32 [1280], P(('dp', 'fsdp'))
- grad_attn_rate: float32 [1280], P(('dp', 'fsdp'))
- grad_mlp_rate: float32 [1280], P(('dp', 'fsdp'))
- grad_up_scale: float32 [5120], P(('dp', 'fsdp'))
- grad_gate_scale: float32 [5120], P(('dp', 'fsdp'))
Inputs may be any that keep to these rules, and one draw needn't show every extreme that they name: `parent_ids`: the blocks form runs of 20 in order; a parent is a block of the same run. Each run holds 1 trees of 20 blocks placed at random: a chain of 8 trunk blocks, four branch blocks whose parent is the trunk's last, and two leaf blocks under each branch; every other block has no parent. `valid_mask`: 1 on a leading part of each block, never empty, 0 after it.
All inputs are finite; a program needn't handle non-finite values.
Results may differ from a plain program's by a relative error of at most 0.017.
Values may be sent and summed in bfloat16 or wider, within the bound.
A program may use at most 576 MiB of HBM per device.

v0:
```python
import math
import jax
import jax.numpy as jnp
from jax import lax
from jax.sharding import PartitionSpec as P

D = 1280
HEADS = 20
HEAD_DIM = 64
FF = 5120
BLOCK = 128
DEPTH = 10
EPS = 1e-06


def unit_rows(vector):
    inverse = lax.rsqrt(jnp.sum(vector * vector, axis=-1, keepdims=True) + EPS)
    return (vector * inverse, inverse)


def unit_back(grad, unit, inverse):
    return (grad - unit * jnp.sum(grad * unit, axis=-1, keepdims=True)) * inverse


def project(left, right):
    return jnp.dot(left, right, preferred_element_type=jnp.float32)


def project_back(grad, weight):
    return jnp.einsum("te,de->td", grad, weight, preferred_element_type=jnp.float32)


def ancestors(local_parent):
    column = jnp.arange(local_parent.shape[0], dtype=jnp.int32)
    columns = [column]
    for depth_step in range(DEPTH - 1):
        column = jnp.where(column >= 0, local_parent[jnp.maximum(column, 0)], -1)
        columns.append(column)
    return jnp.stack(columns, axis=1)


def head_back(grad_flat, unit, inverse, scale):
    scaled = (grad_flat * scale).reshape(unit.shape)
    raw = unit_back(scaled, unit, inverse).reshape(grad_flat.shape)
    scale_grad = jnp.sum(grad_flat * unit.reshape(grad_flat.shape), axis=0)
    return (raw, scale_grad)


def local(
    states,
    teacher,
    parent_ids,
    valid_mask,
    w_query,
    w_key,
    w_value,
    w_out,
    w_up,
    w_gate,
    w_down,
    qk_scale,
    attn_rate,
    mlp_rate,
    up_scale,
    gate_scale,
):
    rows_dev = states.shape[0]
    blocks_dev = rows_dev // BLOCK
    width_rows = w_query.shape[0]
    span = DEPTH * BLOCK
    factor = math.sqrt(HEAD_DIM)
    root_width = math.sqrt(D)
    mask_f = valid_mask.astype(jnp.float32)
    qkv_local = jnp.concatenate((w_query, w_key, w_value), axis=1)
    scal_width_local = jnp.stack((qk_scale, attn_rate, mlp_rate), axis=1)
    piece_qkv = lax.all_gather(qkv_local, ("dp", "fsdp"), axis=0, tiled=True)
    piece_out = lax.all_gather(w_out, ("dp", "fsdp"), axis=0, tiled=True)
    piece_scal = lax.all_gather(scal_width_local, ("dp", "fsdp"), axis=0, tiled=True)
    lefts = states
    total = jnp.dot(lefts, piece_qkv, preferred_element_type=jnp.float32)
    scal_whole = piece_scal
    qkv_raw = total
    scal_width = scal_whole
    scale_qk = scal_width[:, 0].astype(jnp.float32)
    rate_attn = scal_width[:, 1].astype(jnp.float32)
    rate_mlp = scal_width[:, 2].astype(jnp.float32)
    query_raw = qkv_raw[:, :D]
    key_raw = qkv_raw[:, D : 2 * D]
    values = qkv_raw[:, 2 * D :].astype(jnp.bfloat16)
    query_unit, query_inv = unit_rows(query_raw.reshape(rows_dev, HEADS, HEAD_DIM))
    key_unit, key_inv = unit_rows(key_raw.reshape(rows_dev, HEADS, HEAD_DIM))
    query_n = (query_unit.reshape(rows_dev, D) * scale_qk).astype(jnp.bfloat16)
    key_n = (key_unit.reshape(rows_dev, D) * scale_qk).astype(jnp.bfloat16)
    key_group, value_group = (
        lax.all_gather(key_n, "fsdp", axis=0, tiled=True),
        lax.all_gather(values, "fsdp", axis=0, tiled=True),
    )
    group_blocks = parent_ids.shape[0]
    group_base = lax.axis_index("dp") * group_blocks
    local_parent = jnp.where(parent_ids >= 0, parent_ids - group_base, -1)
    paths_all = ancestors(local_parent)
    own_first = lax.axis_index("fsdp") * blocks_dev
    paths = lax.dynamic_slice_in_dim(paths_all, own_first, blocks_dev, 0)
    safe_paths = jnp.maximum(paths, 0)
    key_rows = key_group.reshape(group_blocks, BLOCK, D)[safe_paths].reshape(
        blocks_dev, span, HEADS, HEAD_DIM
    )
    value_rows = value_group.reshape(group_blocks, BLOCK, D)[safe_paths].reshape(
        blocks_dev, span, HEADS, HEAD_DIM
    )
    slot_of = jnp.arange(span, dtype=jnp.int32) // BLOCK
    offset = jnp.arange(span, dtype=jnp.int32) % BLOCK
    row_pos = jnp.arange(BLOCK, dtype=jnp.int32)
    causal = offset[None, :] <= row_pos[:, None]
    is_live = jnp.take(paths, slot_of, axis=1) >= 0
    allowed = jnp.where(slot_of[None, None, :] == 0, causal[None], is_live[:, None, :])[:, None]
    query_heads = query_n.reshape(blocks_dev, BLOCK, HEADS, HEAD_DIM)
    scores = factor * jnp.einsum(
        "bqhd,bkhd->bhqk", query_heads, key_rows, preferred_element_type=jnp.float32
    )
    scores = jnp.where(allowed, scores, jnp.float32(-1e30))
    row_max = jnp.max(scores, axis=-1, keepdims=True)
    powers = jnp.exp(scores - row_max)
    row_sum = jnp.sum(powers, axis=-1, keepdims=True)
    probs_b = (powers / row_sum).astype(jnp.bfloat16)
    log_total = row_max + jnp.log(row_sum)
    mixed = jnp.einsum("bhqk,bkhd->bqhd", probs_b, value_rows, preferred_element_type=jnp.float32)
    mixed = mixed.reshape(rows_dev, D).astype(jnp.bfloat16)
    inputs = states.astype(jnp.float32)
    attn = project(mixed, piece_out)
    attn_unit, attn_inv = unit_rows(attn)
    hidden, hidden_inv = unit_rows(inputs + rate_attn * (attn_unit - inputs))
    hidden_b = hidden.astype(jnp.bfloat16)
    ffn_local = jnp.concatenate((w_up, w_gate), axis=1)
    scal_hidden_local = jnp.concatenate(
        (up_scale.reshape(width_rows, 4), gate_scale.reshape(width_rows, 4)), axis=1
    )
    piece_ffn = lax.all_gather(ffn_local, ("dp", "fsdp"), axis=0, tiled=True)
    piece_scal = lax.all_gather(scal_hidden_local, ("dp", "fsdp"), axis=0, tiled=True)
    lefts = hidden_b
    total = jnp.dot(lefts, piece_ffn, preferred_element_type=jnp.float32)
    scal_whole = piece_scal
    scale_up = scal_whole[:, :4].reshape(FF).astype(jnp.float32)
    scale_gate = scal_whole[:, 4:].reshape(FF).astype(jnp.float32)
    up_proj = total[:, :FF]
    gate_proj = total[:, FF:]
    upscaled = up_proj * scale_up
    gated = gate_proj * scale_gate * root_width
    sigmoid_gate = jax.nn.sigmoid(gated)
    act = (upscaled * (gated * sigmoid_gate)).astype(jnp.bfloat16)
    lefts = act
    down = jnp.dot(
        lefts,
        lax.all_gather(w_down, ("dp", "fsdp"), axis=0, tiled=True),
        preferred_element_type=jnp.float32,
    )
    down_unit, down_inv = unit_rows(down)
    result, result_inv = unit_rows(hidden + rate_mlp * (down_unit - hidden))
    loss_local = jnp.sum(mask_f[:, None] * (result - teacher) ** 2)
    valid_count, loss_sum = lax.psum((jnp.sum(mask_f), loss_local), ("dp", "fsdp"))
    loss = loss_sum / valid_count
    g_result = 2.0 * mask_f[:, None] * (result - teacher) / valid_count
    g_last = unit_back(g_result, result, result_inv)
    g_hidden = g_last * (1.0 - rate_mlp)
    g_rate_mlp = jnp.sum(g_last * (down_unit - hidden), axis=0)
    g_down = unit_back(g_last * rate_mlp, down_unit, down_inv).astype(jnp.bfloat16)
    g_act = jnp.einsum(
        "te,fe->tf",
        g_down,
        lax.all_gather(w_down, ("dp", "fsdp"), axis=0, tiled=True),
        preferred_element_type=jnp.float32,
    )
    g_upscaled = g_act * (gated * sigmoid_gate)
    g_gated = g_act * upscaled * sigmoid_gate * (1.0 + gated * (1.0 - sigmoid_gate))
    grad_up_scale = jnp.sum(g_upscaled * up_proj, axis=0)
    grad_gate_scale = jnp.sum(g_gated * gate_proj * root_width, axis=0)
    g_up = (g_upscaled * scale_up).astype(jnp.bfloat16)
    g_gate = (g_gated * scale_gate * root_width).astype(jnp.bfloat16)
    g_both = jnp.concatenate((g_up, g_gate), axis=1)
    g_hidden = g_hidden + jnp.einsum(
        "tc,dc->td",
        g_both,
        lax.all_gather(ffn_local, ("dp", "fsdp"), axis=0, tiled=True),
        preferred_element_type=jnp.float32,
    )
    scal_terms = jnp.concatenate(
        (grad_up_scale.reshape(D, 4), grad_gate_scale.reshape(D, 4)), axis=1
    )
    lefts = hidden_b
    main = jnp.einsum("td,tc->dc", lefts, g_both, preferred_element_type=jnp.float32)
    ffn_share = lax.psum_scatter(
        jnp.concatenate((main, scal_terms), axis=1), ("dp", "fsdp"), scatter_dimension=0, tiled=True
    )
    lefts = act
    grad_down = lax.psum_scatter(
        jnp.einsum("tf,te->fe", lefts, g_down, preferred_element_type=jnp.float32),
        ("dp", "fsdp"),
        scatter_dimension=0,
        tiled=True,
    )
    g_pre = unit_back(g_hidden, hidden, hidden_inv)
    g_states = g_pre * (1.0 - rate_attn)
    g_rate_attn = jnp.sum(g_pre * (attn_unit - inputs), axis=0)
    g_attn = unit_back(g_pre * rate_attn, attn_unit, attn_inv).astype(jnp.bfloat16)
    g_mixed = project_back(g_attn, piece_out).astype(jnp.bfloat16)
    scores = factor * jnp.einsum(
        "bqhd,bkhd->bhqk", query_heads, key_rows, preferred_element_type=jnp.float32
    )
    probs = jnp.where(allowed, jnp.exp(scores - log_total), jnp.float32(0.0))
    probs_again = probs.astype(jnp.bfloat16)
    g_heads = g_mixed.reshape(blocks_dev, BLOCK, HEADS, HEAD_DIM)
    g_probs = jnp.einsum("bqhd,bkhd->bhqk", g_heads, value_rows, preferred_element_type=jnp.float32)
    delta = jnp.sum(probs * g_probs, axis=-1, keepdims=True)
    g_scores = (probs * (g_probs - delta)).astype(jnp.bfloat16)
    g_query_n = factor * jnp.einsum(
        "bhqk,bkhd->bqhd", g_scores, key_rows, preferred_element_type=jnp.float32
    )
    g_key_rows = factor * jnp.einsum(
        "bhqk,bqhd->bkhd", g_scores, query_heads, preferred_element_type=jnp.float32
    )
    g_value_rows = jnp.einsum(
        "bhqk,bqhd->bkhd", probs_again, g_heads, preferred_element_type=jnp.float32
    )
    flat_paths = safe_paths.reshape(blocks_dev * DEPTH)
    g_key_group = (
        jnp.zeros((group_blocks, BLOCK, D), jnp.float32)
        .at[flat_paths]
        .add(g_key_rows.reshape(blocks_dev * DEPTH, BLOCK, D))
    )
    g_value_group = (
        jnp.zeros((group_blocks, BLOCK, D), jnp.float32)
        .at[flat_paths]
        .add(g_value_rows.reshape(blocks_dev * DEPTH, BLOCK, D))
    )
    g_key_n, g_values = (
        lax.psum_scatter(
            g_key_group.reshape(group_blocks * BLOCK, D).astype(jnp.bfloat16),
            "fsdp",
            scatter_dimension=0,
            tiled=True,
        ).astype(jnp.float32),
        lax.psum_scatter(
            g_value_group.reshape(group_blocks * BLOCK, D).astype(jnp.bfloat16),
            "fsdp",
            scatter_dimension=0,
            tiled=True,
        ).astype(jnp.float32),
    )
    g_query_raw, scale_from_query = head_back(
        g_query_n.reshape(rows_dev, D), query_unit, query_inv, scale_qk
    )
    g_key_raw, scale_from_key = head_back(g_key_n, key_unit, key_inv, scale_qk)
    grad_qk_scale = scale_from_query + scale_from_key
    g_qkv = jnp.concatenate(
        (
            g_query_raw.astype(jnp.bfloat16),
            g_key_raw.astype(jnp.bfloat16),
            g_values.astype(jnp.bfloat16),
        ),
        axis=1,
    )
    g_states = g_states + jnp.einsum(
        "tc,dc->td",
        g_qkv,
        lax.all_gather(qkv_local, ("dp", "fsdp"), axis=0, tiled=True),
        preferred_element_type=jnp.float32,
    )
    vector_terms = jnp.stack((grad_qk_scale, g_rate_attn, g_rate_mlp), axis=1)
    lefts = states
    main = jnp.einsum("td,tc->dc", lefts, g_qkv, preferred_element_type=jnp.float32)
    outer = jnp.einsum("td,tc->dc", mixed, g_attn, preferred_element_type=jnp.float32)
    attn_share = lax.psum_scatter(
        jnp.concatenate((main, outer, vector_terms), axis=1),
        ("dp", "fsdp"),
        scatter_dimension=0,
        tiled=True,
    )
    return (
        result.astype(jnp.bfloat16),
        loss,
        g_states,
        attn_share[:, :D],
        attn_share[:, D : 2 * D],
        attn_share[:, 2 * D : 3 * D],
        attn_share[:, 3 * D : 4 * D],
        ffn_share[:, :FF],
        ffn_share[:, FF : 2 * FF],
        grad_down,
        attn_share[:, 4 * D],
        attn_share[:, 4 * D + 1],
        attn_share[:, 4 * D + 2],
        ffn_share[:, 2 * FF : 2 * FF + 4].reshape(-1),
        ffn_share[:, 2 * FF + 4 : 2 * FF + 8].reshape(-1),
    )


def solution(mesh):
    placed = (
        P(("dp", "fsdp"), None),
        P(("dp", "fsdp"), None),
        P("dp"),
        P(("dp", "fsdp")),
        P(("dp", "fsdp"), None),
        P(("dp", "fsdp"), None),
        P(("dp", "fsdp"), None),
        P(("dp", "fsdp"), None),
        P(("dp", "fsdp"), None),
        P(("dp", "fsdp"), None),
        P(("dp", "fsdp"), None),
        P(("dp", "fsdp")),
        P(("dp", "fsdp")),
        P(("dp", "fsdp")),
        P(("dp", "fsdp")),
        P(("dp", "fsdp")),
    )
    return jax.shard_map(
        local,
        mesh=mesh,
        in_specs=placed,
        out_specs=(
            P(("dp", "fsdp"), None),
            P(),
            P(("dp", "fsdp"), None),
            P(("dp", "fsdp"), None),
            P(("dp", "fsdp"), None),
            P(("dp", "fsdp"), None),
            P(("dp", "fsdp"), None),
            P(("dp", "fsdp"), None),
            P(("dp", "fsdp"), None),
            P(("dp", "fsdp"), None),
            P(("dp", "fsdp")),
            P(("dp", "fsdp")),
            P(("dp", "fsdp")),
            P(("dp", "fsdp")),
            P(("dp", "fsdp")),
        ),
        check_vma=False,
    )
```

profile of v0, /device:TPU:14, one launch (start us, length us, event | category | flops | bytes accessed | tf_op | source)
XLA Modules:
  0.0 2938.8 jit_solution(9725263483345402264)
XLA Ops:
  9.0 86.4 %all-gather.9.cloned.1.call-done = bf16[1280,3840]{1,0:T(8,128)(2,1)} async-done(((bf16[40,3840]{1,0:T(8,128)(2,1)}), bf16[1280,3840]{1,0:T(8,128)(2,1)}) %all-gather.9.cloned.1.call-update) | async-done | bytes 9830416 | tf_op jit(solution)/shard_map/all_gather | solution.py:76
  95.4 11.2 convolution_bitcast_fusion.1
  106.6 3.8 copy-done.2
  111.9 29.3 all-gather
  141.9 5.1 slice_multiply_fusion.1
  147.1 3.4 reduce_sum.198
  150.9 6.5 multiply_convert_fusion.7
  173.8 38.1 %all-gather.1 = bf16[32,40,8]{1,2,0:T(8,128)(2,1)S(1)} all-gather(bf16[1,40,8]{1,2,0:T(8,128)(2,1)S(1)} %maximum_bitcast_fusion), channel_id=1, replica_groups=mesh['dp'=8,'fsdp'=4] {'dp','fsdp'}, dimensions={0}, use_global_device_ids=true | all-gather | bytes 21120 | tf_op jit(solution)/shard_map/all_gather | solution.py:139
  214.5 50.4 %psum.15 = f32[]{:T(128)} all-reduce(f32[]{:T(128)} %get-tuple-element.167), channel_id=1, replica_groups=mesh['dp'=8,'fsdp'=4] {'dp','fsdp'}, use_global_device_ids=true, to_apply=%region_11.12 | all-reduce | flops 1 | bytes 8 | tf_op jit(solution)/shard_map/psum | solution.py:160
  266.3 3.8 reshape.781
  270.1 9.9 copy.194
  280.0 10.6 gather_fusion.9
  290.6 46.2 %reshape.933 = bf16[5,1280,20,64]{3,2,1,0:T(8,128)(2,1)} reshape(bf16[50,128,1280]{2,1,0:T(8,128)(2,1)} %gather_fusion.9) | data formatting | bytes 32768000 | tf_op jit(solution)/shard_map/reshape | solution.py:108
  336.8 47.0 %copy.213 = bf16[5,1280,20,64]{1,3,2,0:T(8,128)(2,1)} copy(bf16[5,1280,20,64]{3,2,1,0:T(8,128)(2,1)} %reshape.933) | data formatting | bytes 32768000 | tf_op jit(solution)/shard_map/reshape | solution.py:108
  383.8 9.5 copy.209
  393.3 10.7 gather_fusion.11
  404.0 46.3 %reshape.934 = bf16[5,1280,20,64]{3,2,1,0:T(8,128)(2,1)} reshape(bf16[50,128,1280]{2,1,0:T(8,128)(2,1)} %gather_fusion.11) | data formatting | bytes 32768000 | tf_op jit(solution)/shard_map/reshape | solution.py:105
  450.4 47.0 %copy.212 = bf16[5,1280,20,64]{1,3,2,0:T(8,128)(2,1)} copy(bf16[5,1280,20,64]{3,2,1,0:T(8,128)(2,1)} %reshape.934) | data formatting | bytes 32768000 | tf_op jit(solution)/shard_map/reshape | solution.py:105
  497.3 30.2 %select_reduce_fusion = (f32[5,20,128]{2,1,0:T(8,128)S(1)}, f32[5,20,128,1280]{3,2,1,0:T(8,128)}) fusion(pred[5,128,1280]{2,1,0:T(8,128)(4,1)S(1)} %broadcast_select_fusion, bf16[5,1280,20,64]{1,3,2,0:T(8,128)(2,1)} %copy.212, bf16[5,128,20,64]{1,0,3,2:T(8,128)(2,1)S(1)} %reshape.781), kind=kOutput, calls=%fused_computation.20 | convolution fusion | flops 2146291200 | bytes 84428800 | tf_op jit(solution)/shard_map/bqhd,bkhd->bhqk/dot_general | solution.py:118
  527.5 21.3 fusion.1
  548.8 31.6 %fusion.32 = bf16[5,128,20,64]{1,3,2,0:T(8,128)(2,1)} fusion(bf16[5,1280,20,64]{1,3,2,0:T(8,128)(2,1)} %copy.213, f32[5,20,128,1280]{3,2,1,0:T(8,128)} %get-tuple-element.169, f32[5,20,128]{2,1,0:T(8,128)S(1)} %fusion.1, f32[5,20,128]{2,1,0:T(8,128)S(1)} %get-tuple-element.168, pred[5,128,1280]{2,1,0:T(8,128)(4,1)S(1)} %broadcast_select_fusion), kind=kOutput, calls=%fused_computation.107 | convolution fusion | flops 2179891200 | bytes 84480000 | tf_op jit(solution)/shard_map/bhqk,bkhd->bqhd/dot_general | solution.py:127
  583.3 5.3 multiply_reduce_fusion.14
  591.0 27.2 fusion.63
  618.3 12.6 multiply_convert_fusion.3
  630.8 13.2 multiply_reduce_fusion.12
  646.0 2.9 multiply_reduce_fusion.9
  648.9 4.6 multiply_reduce_fusion.3
  656.0 29.7 %multiply_reduce_fusion.1 = (f32[5120]{0:T(1024)}, f32[5120]{0:T(1024)}, f32[640,5120]{1,0:T(8,128)}, bf16[640,5120]{1,0:T(8,128)(2,1)}) fusion(f32[640,10240]{1,0:T(8,128)} %fusion.63, f32[5120]{0:T(1024)S(1)} %copy-done.40, f32[5120]{0:T(1024)S(1)} %copy-done.43, bf16[640,1280]{1,0:T(8,128)(2,1)S(1)} %multiply_convert_fusion.5, ...), kind=kOutput, calls=%fused_computation.33 | convolution fusion | flops 8457410560 | bytes 60702720 | tf_op jit(solution)/shard_map/te,fe->tf/dot_general | solution.py:167
  685.7 9.2 multiply_convert_fusion.1
  694.9 26.7 multiply_reduce_fusion.7
  721.6 5.6 multiply_reduce_fusion.4
  733.2 4.3 reshape.935
  737.6 4.6 copy.221
  742.2 55.0 %multiply_reduce_fusion = (f32[5,20,128]{2,1,0:T(8,128)}, f32[5,20,128,1280]{3,2,1,0:T(8,128)}) fusion(f32[5,20,128,1280]{3,2,1,0:T(8,128)} %get-tuple-element.169, f32[5,20,128]{2,1,0:T(8,128)S(1)} %copy-done.32, pred[5,128,1280]{2,1,0:T(8,128)(4,1)S(1)} %copy-done.6, bf16[5,128,20,64]{1,3,2,0:T(8,128)(2,1)S(1)} %copy.221, bf16[5,1280,20,64]{1,3,2,0:T(8,128)(2,1)} %copy.213), kind=kOutput, calls=%fused_computation.16 | convolution fusion | flops 2179059200 | bytes 150016000 | tf_op jit(solution)/shard_map/bqhd,bkhd->bhqk/dot_general | solution.py:212
  797.1 52.9 %multiply_convert_fusion = bf16[5,20,128,1280]{3,2,1,0:T(8,128)(2,1)} fusion(f32[5,20,128,1280]{3,2,1,0:T(8,128)} %get-tuple-element.177, f32[5,20,128,1280]{3,2,1,0:T(8,128)} %get-tuple-element.169, f32[5,20,128]{2,1,0:T(8,128)} %get-tuple-element.176, f32[5,20,128]{2,1,0:T(8,128)S(1)} %copy-done.32, pred[5,128,1280]{2,1,0:T(8,128)(4,1)S(1)} %copy-done.6), kind=kLoop, calls=%fused_computation.15 | loop fusion | flops 98304000 | bytes 164761600 | tf_op jit(solution)/shard_map/convert_element_type | solution.py:214
  850.1 20.9 multiply_bitcast_fusion
  871.0 53.4 %copy.240 = f32[5,1280,20,64]{3,2,1,0:T(8,128)} copy(f32[5,1280,20,64]{1,3,2,0:T(8,128)} %multiply_bitcast_fusion) | data formatting | bytes 65536000 | tf_op jit(solution)/shard_map/reshape | solution.py:228
  924.4 57.4 %reshape.925 = f32[50,128,1280]{2,1,0:T(8,128)} reshape(f32[5,1280,20,64]{3,2,1,0:T(8,128)} %copy.240) | data formatting | bytes 65536000 | tf_op jit(solution)/shard_map/reshape | solution.py:228
  981.8 6.1 broadcast.941.clone.1
  987.9 65.4 %scatter_fusion = f32[20,128,1280]{2,1,0:T(8,128)} fusion(f32[20,128,1280]{2,1,0:T(8,128)} %broadcast.941.clone.1, s32[50]{0:T(128)S(1)} %copy-done.55, f32[50,128,1280]{2,1,0:T(8,128)} %reshape.925), kind=kCustom, calls=%fused_computation.12 | custom fusion | flops 8192000 | bytes 98304200 | tf_op jit(solution)/shard_map/scatter-add | solution.py:228
  1053.2 8.3 convert_element_type.167
  1062.9 38.6 %fusion.10 = f32[5,1280,20,64]{1,3,2,0:T(8,128)} fusion(bf16[5,128,20,64]{1,3,2,0:T(8,128)(2,1)S(1)} %copy-done.12, f32[5,20,128,1280]{3,2,1,0:T(8,128)} %get-tuple-element.169, f32[5,20,128]{2,1,0:T(8,128)S(1)} %copy-done.32, pred[5,128,1280]{2,1,0:T(8,128)(4,1)S(1)} %copy-done.6), kind=kOutput, calls=%fused_computation.30 | convolution fusion | flops 2162688000 | bytes 100812800 | tf_op jit(solution)/shard_map/bhqk,bqhd->bkhd/dot_general | solution.py:221
  1101.5 53.5 %copy.241 = f32[5,1280,20,64]{3,2,1,0:T(8,128)} copy(f32[5,1280,20,64]{1,3,2,0:T(8,128)} %fusion.10) | data formatting | bytes 65536000 | tf_op jit(solution)/shard_map/reshape | solution.py:233
  1155.0 57.4 %reshape.926 = f32[50,128,1280]{2,1,0:T(8,128)} reshape(f32[5,1280,20,64]{3,2,1,0:T(8,128)} %copy.241) | data formatting | bytes 65536000 | tf_op jit(solution)/shard_map/reshape | solution.py:233
  1212.4 6.1 broadcast.941.clone
  1218.5 64.8 %scatter_fusion.1 = f32[20,128,1280]{2,1,0:T(8,128)} fusion(f32[20,128,1280]{2,1,0:T(8,128)} %broadcast.941.clone, s32[50]{0:T(128)S(1)} %copy-done.55, f32[50,128,1280]{2,1,0:T(8,128)} %reshape.926), kind=kCustom, calls=%fused_computation.13 | custom fusion | flops 8192000 | bytes 98304200 | tf_op jit(solution)/shard_map/scatter-add | solution.py:233
  1283.3 8.3 convert_element_type.172
  1293.6 2.9 reshape.789
  1296.5 26.3 fusion.23
  1323.1 4.8 copy.224
  1331.1 31.7 %fusion.14 = f32[1280,10240]{1,0:T(8,128)} fusion(bf16[640,5120]{1,0:T(8,128)(2,1)} %multiply_convert_fusion.1, bf16[640,5120]{1,0:T(8,128)(2,1)} %get-tuple-element.148, f32[640,1280]{1,0:T(8,128)S(1)} %copy-done.1, f32[640]{0:T(1024)S(1)} %copy-done.23), kind=kOutput, calls=%fused_computation.43 | convolution fusion | flops 16805068800 | bytes 68815360 | tf_op jit(solution)/shard_map/td,tc->dc/dot_general | solution.py:190
  1362.8 55.9 %concatenate.27 = f32[1280,10248]{1,0:T(8,128)} concatenate(f32[1280,10240]{1,0:T(8,128)} %fusion.14, f32[1280,4]{1,0:T(8,128)} %reshape.794, f32[1280,4]{1,0:T(8,128)} %reshape.795), dimensions={1} | concatenate | bytes 104939520 | tf_op jit(solution)/shard_map/concatenate | solution.py:192
  1418.8 6.9 fusion.27
  1425.6 2.9 copy.243
  1432.6 6.1 fusion.17
  1438.8 4.5 copy.245
  1443.3 14.7 convolution_bitcast_fusion
  1457.9 60.2 %concatenate.26 = f32[1280,5123]{0,1:T(8,128)} concatenate(f32[1280,3840]{0,1:T(8,128)} %convolution_bitcast_fusion, f32[1280,1280]{0,1:T(8,128)} %fusion.27, f32[1280,1]{0,1:T(1,128)S(1)} %add.198, f32[1280,1]{0,1:T(1,128)S(1)} %stack.40, f32[1280,1]{0,1:T(1,128)S(1)} %stack.41), dimensions={1} | concatenate | bytes 52459520 | tf_op jit(solution)/shard_map/concatenate | solution.py:273
  1519.6 17.0 fusion.67
  1537.2 42.5 %psum.14 = f32[]{:T(128)} all-reduce(f32[]{:T(128)} %get-tuple-element.114), channel_id=1, replica_groups=mesh['dp'=8,'fsdp'=4] {'dp','fsdp'}, use_global_device_ids=true, to_apply=%region_9.10 | all-reduce | flops 1 | bytes 8 | tf_op jit(solution)/shard_map/psum | solution.py:160
  1581.1 13.7 convolution_add_fusion
  1594.8 1048.5 %all-reduce.5.cloned.1.call-done = (f32[1280,5123]{0,1:T(8,128)}, f32[1280,10248]{1,0:T(8,128)}) async-done(((f32[1280,5123]{0,1:T(8,128)}, f32[1280,10248]{1,0:T(8,128)}), (f32[1280,5123]{0,1:T(8,128)}, f32[1280,10248]{1,0:T(8,128)})) %all-reduce.5.cloned.1.call-update) | async-done | bytes 78699536
  2643.3 3.3 fusion.66
  2656.5 273.8 %reduce-scatter.9.cloned.1.call-done = f32[160,1280]{1,0:T(8,128)} async-done(((f32[5120,1280]{1,0:T(8,128)}), f32[160,1280]{1,0:T(8,128)}) %reduce-scatter.9.cloned.1.call-update) | async-done | bytes 819216 | tf_op jit(solution)/shard_map/reduce_scatter | solution.py:195
  (274 shorter events, 63.2 us)
Async XLA Ops:
  7.2 88.3 %all-gather.9.cloned.1.call-start = ((), (), s32[]{:S(2)}) async-start(), calls=%async_computation.3 | async-start | bytes 10137600 | tf_op jit(solution)/shard_map/all_gather | solution.py:76
  9.0 261.1 %all-gather.11.cloned.1.call-start = ((), (), s32[]{:S(2)}) async-start(), calls=%async_computation.4 | async-start | bytes 8192000 | tf_op jit(solution)/shard_map/all_gather | solution.py:96
  106.6 3.8 copy-start.2
  111.8 272.1 %all-gather.13.cloned.1.call-start = ((), (), s32[]{:S(2)}) async-start(), calls=%async_computation.5 | async-start | bytes 8192000 | tf_op jit(solution)/shard_map/all_gather | solution.py:95
  141.9 9.0 copy-start.41
  141.9 122.9 %copy-start.35 = (f32[1280]{0:T(1024)}, f32[1280]{0:T(1024)S(1)}, u32[]{:S(2)}) copy-start(f32[1280]{0:T(1024)S(1)} %get-tuple-element.116) | copy-start | bytes 15364
  147.1 3.8 copy-start.7
  150.5 6.9 copy-start.28
  150.9 6.5 copy-start.30
  150.9 7.2 copy-start.33
  150.9 7.2 copy-start.34
  157.4 2.5 copy-start.52
  157.4 4.3 copy-start.62
  157.4 425.8 %all-gather.15.cloned.1.call-start = ((), (), s32[]{:S(2)}) async-start(), calls=%async_computation.6 | async-start | bytes 3379200 | tf_op jit(solution)/shard_map/all_gather | solution.py:77
  158.0 433.0 %all-gather.17.cloned.1.call-start = ((), (), s32[]{:S(2)}) async-start(), calls=%async_computation.7 | async-start | bytes 27033600 | tf_op jit(solution)/shard_map/all_gather | solution.py:138
  159.0 471.8 %all-gather.19.cloned.1.call-start = ((), (), s32[]{:S(2)}) async-start(), calls=%async_computation.8 | async-start | bytes 13516800 | tf_op jit(solution)/shard_map/all_gather | solution.py:154
  159.6 1266.0 %reduce-scatter.11.cloned.1.call-start = ((), (), s32[]{:S(2)}) async-start(), calls=%async_computation.10 | async-start | bytes 8192000
  162.4 10.9 copy-start.59
  162.4 11.1 copy-start.60
  266.3 282.5 %copy-start.5 = (pred[5,128,1280]{2,1,0:T(8,128)(4,1)}, pred[5,128,1280]{2,1,0:T(8,128)(4,1)S(1)}, u32[]{:S(2)}) copy-start(pred[5,128,1280]{2,1,0:T(8,128)(4,1)S(1)} %broadcast_select_fusion) | copy-start | bytes 2457604
  270.1 227.2 %copy-start.9 = (bf16[5,128,20,64]{1,0,3,2:T(8,128)(2,1)}, bf16[5,128,20,64]{1,0,3,2:T(8,128)(2,1)S(1)}, u32[]{:S(2)}) copy-start(bf16[5,128,20,64]{1,0,3,2:T(8,128)(2,1)S(1)} %reshape.781) | copy-start | bytes 4915204
  583.2 5.4 copy-start.20
  583.3 5.4 copy-start.18
  583.3 5.4 copy-start.37
  590.3 131.2 %copy-start = (f32[640,1280]{1,0:T(8,128)}, f32[640,1280]{1,0:T(8,128)S(1)}, u32[]{:S(2)}) copy-start(f32[640,1280]{1,0:T(8,128)S(1)} %get-tuple-element.127) | copy-start | bytes 9830404
  590.3 131.2 %copy-start.22 = (f32[640]{0:T(1024)}, f32[640]{0:T(1024)S(1)}, u32[]{:S(2)}) copy-start(f32[640]{0:T(1024)S(1)} %add_rsqrt_fusion.4) | copy-start | bytes 7684
  591.0 27.2 copy-start.40
  591.0 27.2 copy-start.43
  630.8 13.2 copy-start.36
  644.1 1.9 copy-start.13
  644.1 1.9 copy-start.46
  644.1 1.9 copy-start.53
  653.6 1.7 copy-start.16
  656.0 29.7 %copy-start.25 = (bf16[640,1280]{1,0:T(8,128)(2,1)}, bf16[640,1280]{1,0:T(8,128)(2,1)S(1)}, u32[]{:S(2)}) copy-start(bf16[640,1280]{1,0:T(8,128)(2,1)S(1)} %multiply_convert_fusion.5) | copy-start | bytes 4915204
  685.7 9.2 copy-start.54
  694.9 26.7 copy-start.38
  694.9 26.7 copy-start.45
  721.6 5.6 copy-start.4
  727.2 1.7 copy-start.14
  727.2 3.7 copy-start.61
  737.6 4.6 copy-start.6
  737.6 4.6 copy-start.32
  742.2 55.0 %copy-start.11 = (bf16[5,128,20,64]{1,3,2,0:T(8,128)(2,1)}, bf16[5,128,20,64]{1,3,2,0:T(8,128)(2,1)S(1)}, u32[]{:S(2)}) copy-start(bf16[5,128,20,64]{1,3,2,0:T(8,128)(2,1)S(1)} %copy.221) | copy-start | bytes 4915204
  797.1 52.9 %copy-start.10 = (bf16[5,128,20,64]{1,0,3,2:T(8,128)(2,1)S(1)}, bf16[5,128,20,64]{1,0,3,2:T(8,128)(2,1)}, u32[]{:S(2)}) copy-start(bf16[5,128,20,64]{1,0,3,2:T(8,128)(2,1)} %copy-done.9) | copy-start | bytes 4915204
  981.8 6.1 copy-start.55
  1061.5 377.2 %reduce-scatter.13.cloned.1.call-start = ((), (), s32[]{:S(2)}) async-start(), calls=%async_computation.11 | async-start | bytes 8192000
  1291.6 2.0 copy-start.17
  1291.6 1351.7 %all-reduce.5.cloned.1.call-start = ((), (), s32[]{:S(2)}) async-start(), calls=%async_computation.12 | async-start | bytes 158679040
  1323.1 5.0 copy-start.48
  1323.1 5.0 copy-start.47
  1323.1 5.0 copy-start.51
  1323.1 6.5 copy-start.50
  1323.1 8.0 copy-start.1
  1323.1 8.0 copy-start.23
  1362.8 55.9 %copy-start.21 = (bf16[5,128,20,64]{1,0,3,2:T(8,128)(2,1)S(1)}, bf16[5,128,20,64]{1,0,3,2:T(8,128)(2,1)}, u32[]{:S(2)}) copy-start(bf16[5,128,20,64]{1,0,3,2:T(8,128)(2,1)} %copy-done.20) | copy-start | bytes 4915204
  1425.6 2.9 copy-start.42
  1428.5 1.9 copy-start.8
  1428.5 1.9 copy-start.31
  1429.0 3.6 slice-start
  1430.4 2.2 slice-start.1
  1438.7 19.2 copy-start.24
  1438.7 4.5 copy-start.19
  1518.2 1412.2 %reduce-scatter.9.cloned.1.call-start = ((), (), s32[]{:S(2)}) async-start(), calls=%async_computation.9 | async-start | bytes 27033600 | tf_op jit(solution)/shard_map/reduce_scatter | solution.py:195
  1536.5 44.5 %copy-start.15 = (f32[640,1280]{1,0:T(8,128)S(1)}, f32[640,1280]{1,0:T(8,128)}, u32[]{:S(2)}) copy-start(f32[640,1280]{1,0:T(8,128)} %copy-done.14) | copy-start | bytes 9830404
  (11 other events, 13.9 us)
Sparse Core Ops, SparseCore 0:
  11.5 83.8 all-gather.8
  111.9 46.6 all-gather.10
  160.2 51.7 all-gather.12
  214.7 58.7 all-gather.14
  276.8 157.2 all-gather.16
  436.8 97.6 all-gather.18
  1061.7 58.2 reduce-scatter.10
  1291.7 59.9 reduce-scatter.12
  1518.3 1124.9 all-reduce.4
  2646.0 284.3 reduce-scatter.8
where the time goes:
time: 2960 us; the launch traced here: 2940 us
  waiting for transfers between devices  1410 us (48%)
  local copies, waits for them, and re-layouts  656 us (22%)
  matrix products  402 us (14%)
  other arithmetic  292 us (10%)
  blocking collectives  160 us (5%)
    unnamed x13, waiting for transfers between devices  1050 us
    reduce_scatter x1, waiting for transfers between devices, local(): lax.psum_scatter(jnp.einsum('tf,te->fe', lefts, g_down, preferred_element...  274 us
    reshape x2, local copies, waits for them, and re-layouts, local(): g_value_rows.reshape(blocks_dev * DEPTH, BLOCK, D)  111 us
    reshape x2, local copies, waits for them, and re-layouts, local(): g_key_rows.reshape(blocks_dev * DEPTH, BLOCK, D)  111 us
    reshape x2, local copies, waits for them, and re-layouts, local(): key_group.reshape(group_blocks, BLOCK, D)[safe_paths]  93.3 us
    reshape x2, local copies, waits for them, and re-layouts, local(): value_group.reshape(group_blocks, BLOCK, D)[safe_paths]  93.2 us
    psum x2, blocking collectives, local(): lax.psum((jnp.sum(mask_f), loss_local), ('dp', 'fsdp'))  92.9 us
    all_gather x1, waiting for transfers between devices, local(): piece_qkv = lax.all_gather(qkv_local, ('dp', 'fsdp'), axis=0, tiled=True)  86.4 us
  transfers between devices with their start and end apart: 10, of which 3 were waited for; matrix products, arithmetic and copies ran while one was open for 28% of the time, Pallas kernels for 0%

commit v1 on v0

--- a/solution.py
+++ b/solution.py
@@ -73,8 +73,13 @@
     mask_f = valid_mask.astype(jnp.float32)
     qkv_local = jnp.concatenate((w_query, w_key, w_value), axis=1)
     scal_width_local = jnp.stack((qk_scale, attn_rate, mlp_rate), axis=1)
-    piece_qkv = lax.all_gather(qkv_local, ("dp", "fsdp"), axis=0, tiled=True)
-    piece_out = lax.all_gather(w_out, ("dp", "fsdp"), axis=0, tiled=True)
+    piece_qkv, piece_out = jnp.split(
+        lax.all_gather(
+            jnp.concatenate([qkv_local, w_out], axis=1), ("dp", "fsdp"), axis=0, tiled=True
+        ),
+        [qkv_local.shape[1]],
+        axis=1,
+    )
     piece_scal = lax.all_gather(scal_width_local, ("dp", "fsdp"), axis=0, tiled=True)
     lefts = states
     total = jnp.dot(lefts, piece_qkv, preferred_element_type=jnp.float32)

time: 2960 us -> 2980 us (level)
  transfers between devices with their start and end apart: 10 -> 10, of which waited for: 3 -> 3; matrix products, arithmetic and copies ran while one was open for 28% -> 30% of each run, Pallas kernels for 0% -> 0%
where the time goes in v1:
time: 2980 us; the launch traced here: 2950 us
  waiting for transfers between devices  1420 us (48%)
  local copies, waits for them, and re-layouts  651 us (22%)
  matrix products  402 us (13%)
  other arithmetic  298 us (10%)
  blocking collectives  160 us (5%)
    unnamed x13, waiting for transfers between devices  1050 us
    reduce_scatter x1, waiting for transfers between devices, local(): lax.psum_scatter(jnp.einsum('tf,te->fe', lefts, g_down, preferred_element...  274 us
    reshape x2, local copies, waits for them, and re-layouts, local(): g_value_rows.reshape(blocks_dev * DEPTH, BLOCK, D)  111 us
    reshape x2, local copies, waits for them, and re-layouts, local(): g_key_rows.reshape(blocks_dev * DEPTH, BLOCK, D)  111 us
    all_gather x1, waiting for transfers between devices, local(): lax.all_gather(jnp.concatenate([qkv_local, w_out], axis=1), ('dp', 'fsdp'...  100 us
    reshape x2, local copies, waits for them, and re-layouts, local(): value_group.reshape(group_blocks, BLOCK, D)[safe_paths]  93.2 us
    reshape x2, local copies, waits for them, and re-layouts, local(): key_group.reshape(group_blocks, BLOCK, D)[safe_paths]  92.8 us
    psum x2, blocking collectives, local(): lax.psum((jnp.sum(mask_f), loss_local), ('dp', 'fsdp'))  92.4 us
  transfers between devices with their start and end apart: 10, of which 3 were waited for; matrix products, arithmetic and copies ran while one was open for 30% of the time, Pallas kernels for 0%

profile of v1, /device:TPU:14, one launch (start us, length us, event | category | flops | bytes accessed | tf_op | source)
XLA Modules:
  0.0 2953.9 jit_solution(10457363003389133343)
XLA Ops:
  9.1 100.3 %all-gather.9.cloned.1.call-done = bf16[1280,5120]{1,0:T(8,128)(2,1)} async-done(((bf16[40,5120]{1,0:T(8,128)(2,1)}), bf16[1280,5120]{1,0:T(8,128)(2,1)}) %all-gather.9.cloned.1.call-update) | async-done | bytes 13107216 | tf_op jit(solution)/shard_map/all_gather | solution.py:77
  109.5 11.0 fusion.18
  120.5 3.8 copy-done.2
  125.7 29.6 %all-gather = bf16[32,40,3]{1,2,0:T(4,128)(2,1)S(1)} all-gather(bf16[1,40,3]{1,2,0:T(4,128)(2,1)S(1)} %maximum_bitcast_fusion.1), channel_id=1, replica_groups=mesh['dp'=8,'fsdp'=4] {'dp','fsdp'}, dimensions={0}, use_global_device_ids=true | all-gather | bytes 7920 | tf_op jit(solution)/shard_map/all_gather | solution.py:83
  156.1 5.1 slice_multiply_fusion.1
  161.2 3.4 reduce_sum.198
  165.0 6.5 multiply_convert_fusion.7
  188.5 38.1 %all-gather.1 = bf16[32,40,8]{1,2,0:T(8,128)(2,1)S(1)} all-gather(bf16[1,40,8]{1,2,0:T(8,128)(2,1)S(1)} %maximum_bitcast_fusion), channel_id=1, replica_groups=mesh['dp'=8,'fsdp'=4] {'dp','fsdp'}, dimensions={0}, use_global_device_ids=true | all-gather | bytes 21120 | tf_op jit(solution)/shard_map/all_gather | solution.py:144
  229.1 50.5 %psum.15 = f32[]{:T(128)} all-reduce(f32[]{:T(128)} %get-tuple-element.167), channel_id=1, replica_groups=mesh['dp'=8,'fsdp'=4] {'dp','fsdp'}, use_global_device_ids=true, to_apply=%region_11.12 | all-reduce | flops 1 | bytes 8 | tf_op jit(solution)/shard_map/psum | solution.py:165
  281.1 3.8 reshape.781
  284.9 9.9 copy.194
  294.8 10.6 gather_fusion.9
  305.4 46.4 %reshape.933 = bf16[5,1280,20,64]{3,2,1,0:T(8,128)(2,1)} reshape(bf16[50,128,1280]{2,1,0:T(8,128)(2,1)} %gather_fusion.9) | data formatting | bytes 32768000 | tf_op jit(solution)/shard_map/reshape | solution.py:113
  351.8 46.9 %copy.213 = bf16[5,1280,20,64]{1,3,2,0:T(8,128)(2,1)} copy(bf16[5,1280,20,64]{3,2,1,0:T(8,128)(2,1)} %reshape.933) | data formatting | bytes 32768000 | tf_op jit(solution)/shard_map/reshape | solution.py:113
  398.6 9.6 copy.209
  408.2 10.6 gather_fusion.11
  418.8 46.3 %reshape.934 = bf16[5,1280,20,64]{3,2,1,0:T(8,128)(2,1)} reshape(bf16[50,128,1280]{2,1,0:T(8,128)(2,1)} %gather_fusion.11) | data formatting | bytes 32768000 | tf_op jit(solution)/shard_map/reshape | solution.py:110
  465.1 46.6 %copy.212 = bf16[5,1280,20,64]{1,3,2,0:T(8,128)(2,1)} copy(bf16[5,1280,20,64]{3,2,1,0:T(8,128)(2,1)} %reshape.934) | data formatting | bytes 32768000 | tf_op jit(solution)/shard_map/reshape | solution.py:110
  511.7 29.2 select_reduce_fusion
  540.9 20.8 fusion.1
  561.8 30.6 %fusion.39 = bf16[5,128,20,64]{1,3,2,0:T(8,128)(2,1)S(1)} fusion(bf16[5,1280,20,64]{1,3,2,0:T(8,128)(2,1)} %copy.213, f32[5,20,128,1280]{3,2,1,0:T(8,128)} %get-tuple-element.169, f32[5,20,128]{2,1,0:T(8,128)S(1)} %fusion.1, f32[5,20,128]{2,1,0:T(8,128)S(1)} %get-tuple-element.168, pred[5,128,1280]{2,1,0:T(8,128)(4,1)S(1)} %broadcast_select_fusion), kind=kOutput, calls=%fused_computation.111 | convolution fusion | flops 2179891200 | bytes 84480000 | tf_op jit(solution)/shard_map/bhqk,bkhd->bqhd/dot_general | solution.py:132
  593.9 5.3 multiply_reduce_fusion.14
  601.6 27.2 fusion.70
  628.9 12.5 multiply_convert_fusion.3
  641.4 13.2 multiply_reduce_fusion.12
  656.5 2.9 multiply_reduce_fusion.9
  659.5 4.6 multiply_reduce_fusion.3
  666.5 29.6 %multiply_reduce_fusion.1 = (f32[5120]{0:T(1024)}, f32[5120]{0:T(1024)}, f32[640,5120]{1,0:T(8,128)}, bf16[640,5120]{1,0:T(8,128)(2,1)}) fusion(f32[640,10240]{1,0:T(8,128)} %fusion.70, f32[5120]{0:T(1024)S(1)} %copy-done.40, f32[5120]{0:T(1024)S(1)} %copy-done.43, bf16[640,1280]{1,0:T(8,128)(2,1)S(1)} %multiply_convert_fusion.5, ...), kind=kOutput, calls=%fused_computation.33 | convolution fusion | flops 8457410560 | bytes 60702720 | tf_op jit(solution)/shard_map/te,fe->tf/dot_general | solution.py:172
  696.1 9.1 multiply_convert_fusion.1
  705.3 26.6 multiply_reduce_fusion.7
  731.9 5.6 multiply_reduce_fusion.4
  740.4 4.2 convolution_convert_fusion
  744.7 4.3 reshape.935
  749.0 4.6 copy.221
  753.6 55.0 %multiply_reduce_fusion = (f32[5,20,128]{2,1,0:T(8,128)}, f32[5,20,128,1280]{3,2,1,0:T(8,128)}) fusion(f32[5,20,128,1280]{3,2,1,0:T(8,128)} %get-tuple-element.169, f32[5,20,128]{2,1,0:T(8,128)S(1)} %copy-done.32, pred[5,128,1280]{2,1,0:T(8,128)(4,1)S(1)} %copy-done.6, bf16[5,128,20,64]{1,3,2,0:T(8,128)(2,1)S(1)} %copy.221, bf16[5,1280,20,64]{1,3,2,0:T(8,128)(2,1)} %copy.213), kind=kOutput, calls=%fused_computation.16 | convolution fusion | flops 2179059200 | bytes 150016000 | tf_op jit(solution)/shard_map/bqhd,bkhd->bhqk/dot_general | solution.py:217
  808.6 52.9 %multiply_convert_fusion = bf16[5,20,128,1280]{3,2,1,0:T(8,128)(2,1)} fusion(f32[5,20,128,1280]{3,2,1,0:T(8,128)} %get-tuple-element.177, f32[5,20,128,1280]{3,2,1,0:T(8,128)} %get-tuple-element.169, f32[5,20,128]{2,1,0:T(8,128)} %get-tuple-element.176, f32[5,20,128]{2,1,0:T(8,128)S(1)} %copy-done.32, pred[5,128,1280]{2,1,0:T(8,128)(4,1)S(1)} %copy-done.6), kind=kLoop, calls=%fused_computation.15 | loop fusion | flops 98304000 | bytes 164761600 | tf_op jit(solution)/shard_map/convert_element_type | solution.py:219
  861.5 20.9 multiply_bitcast_fusion
  882.4 53.4 %copy.240 = f32[5,1280,20,64]{3,2,1,0:T(8,128)} copy(f32[5,1280,20,64]{1,3,2,0:T(8,128)} %multiply_bitcast_fusion) | data formatting | bytes 65536000 | tf_op jit(solution)/shard_map/reshape | solution.py:233
  935.8 57.4 %reshape.925 = f32[50,128,1280]{2,1,0:T(8,128)} reshape(f32[5,1280,20,64]{3,2,1,0:T(8,128)} %copy.240) | data formatting | bytes 65536000 | tf_op jit(solution)/shard_map/reshape | solution.py:233
  993.2 6.1 broadcast.941.clone.1
  999.3 65.4 %scatter_fusion = f32[20,128,1280]{2,1,0:T(8,128)} fusion(f32[20,128,1280]{2,1,0:T(8,128)} %broadcast.941.clone.1, s32[50]{0:T(128)S(1)} %copy-done.55, f32[50,128,1280]{2,1,0:T(8,128)} %reshape.925), kind=kCustom, calls=%fused_computation.12 | custom fusion | flops 8192000 | bytes 98304200 | tf_op jit(solution)/shard_map/scatter-add | solution.py:233
  1064.7 8.4 convert_element_type.167
  1074.5 39.3 %fusion.10 = f32[5,1280,20,64]{1,3,2,0:T(8,128)} fusion(bf16[5,128,20,64]{1,3,2,0:T(8,128)(2,1)S(1)} %copy-done.12, f32[5,20,128,1280]{3,2,1,0:T(8,128)} %get-tuple-element.169, f32[5,20,128]{2,1,0:T(8,128)S(1)} %copy-done.32, pred[5,128,1280]{2,1,0:T(8,128)(4,1)S(1)} %copy-done.6), kind=kOutput, calls=%fused_computation.30 | convolution fusion | flops 2162688000 | bytes 100812800 | tf_op jit(solution)/shard_map/bhqk,bqhd->bkhd/dot_general | solution.py:226
  1113.8 53.4 %copy.241 = f32[5,1280,20,64]{3,2,1,0:T(8,128)} copy(f32[5,1280,20,64]{1,3,2,0:T(8,128)} %fusion.10) | data formatting | bytes 65536000 | tf_op jit(solution)/shard_map/reshape | solution.py:238
  1167.3 57.4 %reshape.926 = f32[50,128,1280]{2,1,0:T(8,128)} reshape(f32[5,1280,20,64]{3,2,1,0:T(8,128)} %copy.241) | data formatting | bytes 65536000 | tf_op jit(solution)/shard_map/reshape | solution.py:238
  1224.7 6.1 broadcast.941.clone
  1230.8 64.8 %scatter_fusion.1 = f32[20,128,1280]{2,1,0:T(8,128)} fusion(f32[20,128,1280]{2,1,0:T(8,128)} %broadcast.941.clone, s32[50]{0:T(128)S(1)} %copy-done.55, f32[50,128,1280]{2,1,0:T(8,128)} %reshape.926), kind=kCustom, calls=%fused_computation.13 | custom fusion | flops 8192000 | bytes 98304200 | tf_op jit(solution)/shard_map/scatter-add | solution.py:238
  1295.5 8.4 convert_element_type.172
  1309.7 25.3 fusion.28
  1335.4 4.9 copy.224
  1343.5 31.9 %fusion.16 = f32[1280,10240]{1,0:T(8,128)} fusion(bf16[640,5120]{1,0:T(8,128)(2,1)} %multiply_convert_fusion.1, bf16[640,5120]{1,0:T(8,128)(2,1)} %get-tuple-element.148, f32[640,1280]{1,0:T(8,128)S(1)} %copy-done.1, f32[640]{0:T(1024)S(1)} %copy-done.23), kind=kOutput, calls=%fused_computation.45 | convolution fusion | flops 16805068800 | bytes 68815360 | tf_op jit(solution)/shard_map/td,tc->dc/dot_general | solution.py:195
  1375.3 56.2 %concatenate.32 = f32[1280,10248]{1,0:T(8,128)} concatenate(f32[1280,10240]{1,0:T(8,128)} %fusion.16, f32[1280,4]{1,0:T(8,128)} %reshape.794, f32[1280,4]{1,0:T(8,128)} %reshape.795), dimensions={1} | concatenate | bytes 104939520 | tf_op jit(solution)/shard_map/concatenate | solution.py:197
  1431.5 6.9 fusion.35
  1438.5 3.7 copy.243
  1446.5 7.1 fusion.22
  1453.7 4.1 copy.245
  1457.8 14.7 convolution_bitcast_fusion
  1472.4 60.2 %concatenate.31 = f32[1280,5123]{0,1:T(8,128)} concatenate(f32[1280,3840]{0,1:T(8,128)} %convolution_bitcast_fusion, f32[1280,1280]{0,1:T(8,128)} %fusion.35, f32[1280,1]{0,1:T(1,128)S(1)} %add.198, f32[1280,1]{0,1:T(1,128)S(1)} %stack.40, f32[1280,1]{0,1:T(1,128)S(1)} %stack.41), dimensions={1} | concatenate | bytes 52459520 | tf_op jit(solution)/shard_map/concatenate | solution.py:278
  1534.1 17.0 fusion.74
  1551.7 42.0 %psum.14 = f32[]{:T(128)} all-reduce(f32[]{:T(128)} %get-tuple-element.114), channel_id=1, replica_groups=mesh['dp'=8,'fsdp'=4] {'dp','fsdp'}, use_global_device_ids=true, to_apply=%region_9.10 | all-reduce | flops 1 | bytes 8 | tf_op jit(solution)/shard_map/psum | solution.py:165
  1595.1 13.8 convolution_add_fusion
  1608.9 1049.5 %all-reduce.5.cloned.1.call-done = (f32[1280,5123]{0,1:T(8,128)}, f32[1280,10248]{1,0:T(8,128)}) async-done(((f32[1280,5123]{0,1:T(8,128)}, f32[1280,10248]{1,0:T(8,128)}), (f32[1280,5123]{0,1:T(8,128)}, f32[1280,10248]{1,0:T(8,128)})) %all-reduce.5.cloned.1.call-update) | async-done | bytes 78699536
  2658.4 3.3 fusion.73
  2671.7 273.8 %reduce-scatter.9.cloned.1.call-done = f32[160,1280]{1,0:T(8,128)} async-done(((f32[5120,1280]{1,0:T(8,128)}), f32[160,1280]{1,0:T(8,128)}) %reduce-scatter.9.cloned.1.call-update) | async-done | bytes 819216 | tf_op jit(solution)/shard_map/reduce_scatter | solution.py:200
  (273 shorter events, 63.4 us)
Async XLA Ops:
  7.2 102.3 %all-gather.9.cloned.1.call-start = ((), (), s32[]{:S(2)}) async-start(), calls=%async_computation.3 | async-start | bytes 13516800 | tf_op jit(solution)/shard_map/all_gather | solution.py:77
  9.1 275.8 %all-gather.11.cloned.1.call-start = ((), (), s32[]{:S(2)}) async-start(), calls=%async_computation.4 | async-start | bytes 8192000 | tf_op jit(solution)/shard_map/all_gather | solution.py:101
  120.5 3.8 copy-start.2
  125.7 273.0 %all-gather.13.cloned.1.call-start = ((), (), s32[]{:S(2)}) async-start(), calls=%async_computation.5 | async-start | bytes 8192000 | tf_op jit(solution)/shard_map/all_gather | solution.py:100
  156.1 8.9 copy-start.41
  156.1 123.5 %copy-start.35 = (f32[1280]{0:T(1024)}, f32[1280]{0:T(1024)S(1)}, u32[]{:S(2)}) copy-start(f32[1280]{0:T(1024)S(1)} %get-tuple-element.116) | copy-start | bytes 15364
  161.2 10.3 copy-start.7
  164.6 6.9 copy-start.28
  165.0 6.5 copy-start.30
  171.5 3.1 copy-start.52
  171.5 4.9 copy-start.61
  171.5 430.1 %all-gather.15.cloned.1.call-start = ((), (), s32[]{:S(2)}) async-start(), calls=%async_computation.6 | async-start | bytes 27033600 | tf_op jit(solution)/shard_map/all_gather | solution.py:143
  173.7 14.3 copy-start.59
  173.7 14.5 copy-start.60
  173.7 467.7 %all-gather.17.cloned.1.call-start = ((), (), s32[]{:S(2)}) async-start(), calls=%async_computation.7 | async-start | bytes 13516800 | tf_op jit(solution)/shard_map/all_gather | solution.py:159
  174.3 1264.2 %reduce-scatter.11.cloned.1.call-start = ((), (), s32[]{:S(2)}) async-start(), calls=%async_computation.10 | async-start | bytes 8192000
  281.1 280.7 %copy-start.5 = (pred[5,128,1280]{2,1,0:T(8,128)(4,1)}, pred[5,128,1280]{2,1,0:T(8,128)(4,1)S(1)}, u32[]{:S(2)}) copy-start(pred[5,128,1280]{2,1,0:T(8,128)(4,1)S(1)} %broadcast_select_fusion) | copy-start | bytes 2457604
  284.9 226.8 %copy-start.9 = (bf16[5,128,20,64]{1,0,3,2:T(8,128)(2,1)}, bf16[5,128,20,64]{1,0,3,2:T(8,128)(2,1)S(1)}, u32[]{:S(2)}) copy-start(bf16[5,128,20,64]{1,0,3,2:T(8,128)(2,1)S(1)} %reshape.781) | copy-start | bytes 4915204
  593.8 5.4 copy-start.20
  593.9 5.4 copy-start.18
  593.9 5.4 copy-start.37
  599.2 1.7 copy-start.3
  599.2 1.7 copy-start.44
  600.9 131.0 %copy-start = (f32[640,1280]{1,0:T(8,128)}, f32[640,1280]{1,0:T(8,128)S(1)}, u32[]{:S(2)}) copy-start(f32[640,1280]{1,0:T(8,128)S(1)} %get-tuple-element.127) | copy-start | bytes 9830404
  600.9 131.0 %copy-start.22 = (f32[640]{0:T(1024)}, f32[640]{0:T(1024)S(1)}, u32[]{:S(2)}) copy-start(f32[640]{0:T(1024)S(1)} %add_rsqrt_fusion.4) | copy-start | bytes 7684
  601.6 27.2 copy-start.40
  601.6 27.2 copy-start.43
  641.4 13.2 copy-start.36
  654.6 1.9 copy-start.13
  654.6 1.9 copy-start.46
  654.6 1.9 copy-start.53
  664.1 1.7 copy-start.16
  666.5 29.7 %copy-start.25 = (bf16[640,1280]{1,0:T(8,128)(2,1)}, bf16[640,1280]{1,0:T(8,128)(2,1)S(1)}, u32[]{:S(2)}) copy-start(bf16[640,1280]{1,0:T(8,128)(2,1)S(1)} %multiply_convert_fusion.5) | copy-start | bytes 4915204
  696.1 9.1 copy-start.54
  705.3 26.6 copy-start.38
  705.3 26.6 copy-start.45
  731.9 5.6 copy-start.4
  749.0 4.6 copy-start.6
  749.0 4.6 copy-start.32
  753.6 55.0 %copy-start.11 = (bf16[5,128,20,64]{1,3,2,0:T(8,128)(2,1)}, bf16[5,128,20,64]{1,3,2,0:T(8,128)(2,1)S(1)}, u32[]{:S(2)}) copy-start(bf16[5,128,20,64]{1,3,2,0:T(8,128)(2,1)S(1)} %copy.221) | copy-start | bytes 4915204
  808.6 52.9 %copy-start.10 = (bf16[5,128,20,64]{1,0,3,2:T(8,128)(2,1)S(1)}, bf16[5,128,20,64]{1,0,3,2:T(8,128)(2,1)}, u32[]{:S(2)}) copy-start(bf16[5,128,20,64]{1,0,3,2:T(8,128)(2,1)} %copy-done.9) | copy-start | bytes 4915204
  993.2 6.1 copy-start.55
  1073.1 380.6 %reduce-scatter.13.cloned.1.call-start = ((), (), s32[]{:S(2)}) async-start(), calls=%async_computation.11 | async-start | bytes 8192000
  1303.9 2.8 copy-start.49
  1303.9 2.9 copy-start.29
  1303.9 2.9 copy-start.17
  1303.9 291.1 %all-gather.19.cloned.1.call-start = ((), (), s32[]{:S(2)}) async-start(), calls=%async_computation.8 | async-start | bytes 10137600 | tf_op jit(solution)/shard_map/all_gather | solution.py:270
  1306.7 1351.8 %all-reduce.5.cloned.1.call-start = ((), (), s32[]{:S(2)}) async-start(), calls=%async_computation.12 | async-start | bytes 158679040
  1335.4 5.0 copy-start.48
  1335.4 5.0 copy-start.47
  1335.4 5.0 copy-start.51
  1335.4 6.5 copy-start.50
  1335.4 8.0 copy-start.1
  1335.4 8.0 copy-start.23
  1375.3 56.2 %copy-start.21 = (bf16[5,128,20,64]{1,0,3,2:T(8,128)(2,1)S(1)}, bf16[5,128,20,64]{1,0,3,2:T(8,128)(2,1)}, u32[]{:S(2)}) copy-start(bf16[5,128,20,64]{1,0,3,2:T(8,128)(2,1)} %copy-done.20) | copy-start | bytes 4915204
  1431.5 10.7 copy-start.42
  1438.5 5.9 copy-start.8
  1438.5 5.9 copy-start.31
  1442.2 4.3 slice-start
  1444.4 2.2 slice-start.1
  1446.5 11.2 copy-start.19
  1453.7 18.8 copy-start.24
  1532.7 1412.9 %reduce-scatter.9.cloned.1.call-start = ((), (), s32[]{:S(2)}) async-start(), calls=%async_computation.9 | async-start | bytes 27033600 | tf_op jit(solution)/shard_map/reduce_scatter | solution.py:200
  1551.0 44.0 %copy-start.15 = (f32[640,1280]{1,0:T(8,128)S(1)}, f32[640,1280]{1,0:T(8,128)}, u32[]{:S(2)}) copy-start(f32[640,1280]{1,0:T(8,128)} %copy-done.14) | copy-start | bytes 9830404
  (10 other events, 12.6 us)
Sparse Core Ops, SparseCore 0:
  11.4 97.9 all-gather.8
  125.8 46.9 all-gather.10
  174.3 51.7 all-gather.12
  229.3 159.0 all-gather.14
  391.2 97.8 all-gather.16
  1073.2 58.5 reduce-scatter.10
  1304.0 59.3 reduce-scatter.12
  1366.9 83.7 all-gather.18
  1532.8 1125.5 all-reduce.4
  2661.2 284.3 reduce-scatter.8
